TPU v7x, 32 devices: a whole 2x2x4 slice. The times are simulated.
32 devices in a mesh: groups: 2 (over x), dp: 16 (over z, y, core).
Axes of the slice: x: 2, y: 2, z: 4, core: 2. Of those that a mesh axis runs over, the one named last changes fastest.
Arguments:
- tokens: bfloat16 [24576, 1024], P(('groups', 'dp')), parts along dimension 0, may hold values from -6 to 6
- token_mask: int32 [32, 768], P(('groups', 'dp')), parts along dimension 0, may hold values 0 or 1
- span_ids: int32 [32, 768], P(('groups', 'dp')), parts along dimension 0, may hold values from 0 to 191, never falling along the last dimension, each value on 1 to 8 neighbouring positions
- norm_gain: float32 [1024], replicated, may hold values from 0.1 to 1.9
- norm_shift: float32 [1024], replicated, may hold values from -3 to 3
- w_up: bfloat16 [1024, 4096], P(None, 'dp'), may hold values from -0.1875 to 0.1875
- b_up: float32 [4096], replicated, may hold values from -3 to 3
- w_down: bfloat16 [4096, 1024], P(None, 'dp'), may hold values from -0.09375 to 0.09375
Outputs:
- whitened: float32 [6144, 1024], P(('groups', 'dp')), parts along dimension 0
There are 2 independent parts, one for each index of `groups`. A program takes and returns all parts, laid end to end along the dimension named above; an argument that names none is the same for every part. Nothing has to cross between parts.
Inputs may be any that keep to these rules, and one draw needn't show every extreme that they name: `span_ids`: in each row the span numbers never fall, every span 0 to 191 holds 1 to 8 tokens, and one holds exactly 8.
All inputs are finite; a program needn't handle non-finite values. No bound on the sum of `token_mask` on one device may be relied on, other than what follows from the above.
Results may differ from a plain program's by a relative error of at most 0.0095.
Values may be sent and summed in bfloat16 or wider, within the bound.
A program may use at most 128 MiB of HBM per device.

v0:
```python
import math
import jax
import jax.numpy as jnp
from jax import lax
from jax.sharding import PartitionSpec as P

SEG_DEV = 192


def on_device(tokens, token_mask, span_ids, norm_gain, norm_shift, w_up, b_up, w_down):
    values = tokens.astype(jnp.float32)
    center = jnp.mean(values, axis=1, keepdims=True)
    spread = jnp.mean((values - center) ** 2, axis=1, keepdims=True)
    normed = ((values - center) * lax.rsqrt(spread + 1e-05) * norm_gain + norm_shift).astype(
        jnp.bfloat16
    )
    up_full, down_full = (
        lax.all_gather(w_up, "dp", axis=1, tiled=True),
        lax.all_gather(w_down, "dp", axis=1, tiled=True),
    )
    before = jnp.dot(normed, up_full, preferred_element_type=jnp.float32) + b_up
    hidden = jax.nn.gelu(before, approximate=False).astype(jnp.bfloat16)
    projected = jnp.dot(hidden, down_full, preferred_element_type=jnp.float32)
    block_out = (values + projected).astype(jnp.bfloat16)
    labels = jnp.arange(SEG_DEV, dtype=jnp.int32)[:, None]
    select = (span_ids[0][None, :] == labels) & (token_mask[0][None, :] == 1)
    sums = jnp.dot(select.astype(jnp.bfloat16), block_out, preferred_element_type=jnp.float32)
    counts = jnp.sum(select.astype(jnp.float32), axis=1)
    pooled = (sums / jnp.maximum(counts, 1.0)[:, None]).astype(jnp.bfloat16)
    partial_gram = jnp.dot(pooled.T, pooled, preferred_element_type=jnp.float32)
    gram = lax.psum(partial_gram, "dp")
    lower = jnp.linalg.cholesky(gram)
    solved = jax.scipy.linalg.solve_triangular(lower, pooled.astype(jnp.float32).T, lower=True)
    total_rows = SEG_DEV * lax.axis_size("dp")
    return math.sqrt(total_rows) * solved.T


def solution(mesh):
    in_specs = (
        P(("groups", "dp"), None),
        P(("groups", "dp"), None),
        P(("groups", "dp"), None),
        P(),
        P(),
        P(None, "dp"),
        P(),
        P(None, "dp"),
    )
    out_specs = P(("groups", "dp"), None)
    return jax.shard_map(
        on_device, mesh=mesh, in_specs=in_specs, out_specs=out_specs, check_vma=False
    )
```

profile of v0, /device:TPU:0, one launch (start us, length us, event | category | flops | bytes accessed | tf_op | source)
XLA Modules:
  0.0 630.8 jit_solution(12674228877443732165)
XLA Ops:
  13.3 77.0 %all-gather.3.cloned.1.call-done = bf16[1024,4096]{1,0:T(8,128)(2,1)} async-done(((bf16[1024,256]{1,0:T(8,128)(2,1)}), bf16[1024,4096]{1,0:T(8,128)(2,1)}) %all-gather.3.cloned.1.call-update) | async-done | bytes 8388624 | tf_op jit(solution)/shard_map/all_gather | solution.py:18
  90.4 37.2 %fusion.2.clone.6 = bf16[768,4096]{1,0:T(8,128)(2,1)} fusion(bf16[1024,4096]{1,0:T(8,128)(2,1)} %all-gather.3.cloned.1.call-done, f32[4096]{0:T(1024)S(1)} %copy-done.2, bf16[768,1024]{1,0:T(8,128)(2,1)S(1)} %copy-done.1, f32[1024]{0:T(1024)S(1)} %copy-done.3, f32[1024]{0:T(1024)S(1)} %copy-done.4, ...), kind=kOutput, calls=%fused_computation.5.clone.clone.clone.clone.clone.1 | convolution fusion | flops 6654787584 | bytes 16283648 | tf_op jit(solution)/shard_map/dot_general | solution.py:21
  127.5 38.1 %all-gather.5.cloned.1.call-done = bf16[4096,1024]{0,1:T(8,128)(2,1)} async-done(((bf16[4096,64]{0,1:T(8,128)(2,1)}), bf16[4096,1024]{0,1:T(8,128)(2,1)}) %all-gather.5.cloned.1.call-update) | async-done | bytes 8388624 | tf_op jit(solution)/shard_map/all_gather | solution.py:19
  165.6 11.2 %fusion.49 = bf16[768,1024]{1,0:T(8,128)(2,1)S(1)} fusion(bf16[768,1024]{1,0:T(8,128)(2,1)S(1)} %copy-done.1, bf16[4096,1024]{0,1:T(8,128)(2,1)} %all-gather.5.cloned.1.call-done, bf16[768,4096]{1,0:T(8,128)(2,1)} %fusion.2.clone.6), kind=kOutput, calls=%fused_computation.66 | convolution fusion | flops 6444810240 | bytes 17825792 | tf_op jit(solution)/shard_map/dot_general | solution.py:23
  180.0 109.8 %all-reduce.3.cloned.1.call-done = f32[1024,1024]{0,1:T(8,128)} async-done(((f32[1024,1024]{0,1:T(8,128)}), f32[1024,1024]{0,1:T(8,128)}) %all-reduce.3.cloned.1.call-update) | async-done | bytes 4194320 | tf_op jit(solution)/shard_map/psum | solution.py:31
  289.9 5.3 copy.12
  301.6 11.7 %cholesky.223 = f32[128,128]{1,0:T(8,128)S(1)} custom-call(f32[128,128]{1,0:T(8,128)S(1)} %cholesky.580), custom_call_target="Cholesky" | custom-call | tf_op jit(solution)/shard_map/jit(cholesky)/cholesky | solution.py:32
  313.3 9.8 %custom-call.63 = f32[1,128,128]{1,2,0:T(8,128)S(1)} custom-call(f32[1,128,128]{2,1,0:T(8,128)S(1)} %get-tuple-element.69), custom_call_target="InvertDiagBlocksLowerTriangular" | custom-call | tf_op jit(solution)/shard_map/jit(cholesky)/cholesky | solution.py:32
  329.6 12.1 %cholesky.244 = f32[128,128]{1,0:T(8,128)S(1)} custom-call(f32[128,128]{1,0:T(8,128)S(1)} %cholesky.584), custom_call_target="Cholesky" | custom-call | tf_op jit(solution)/shard_map/jit(cholesky)/cholesky | solution.py:32
  342.3 9.8 %custom-call.64 = f32[1,128,128]{1,2,0:T(8,128)S(1)} custom-call(f32[1,128,128]{2,1,0:T(8,128)S(1)} %get-tuple-element.66), custom_call_target="InvertDiagBlocksLowerTriangular" | custom-call | tf_op jit(solution)/shard_map/jit(cholesky)/cholesky | solution.py:32
  355.5 11.7 %cholesky.468 = f32[128,128]{1,0:T(8,128)S(1)} custom-call(f32[128,128]{1,0:T(8,128)S(1)} %cholesky.589), custom_call_target="Cholesky" | custom-call | tf_op jit(solution)/shard_map/jit(cholesky)/cholesky | solution.py:32
  368.5 9.8 %custom-call.65 = f32[1,128,128]{1,2,0:T(8,128)S(1)} custom-call(f32[1,128,128]{2,1,0:T(8,128)S(1)} %get-tuple-element.63), custom_call_target="InvertDiagBlocksLowerTriangular" | custom-call | tf_op jit(solution)/shard_map/jit(cholesky)/cholesky | solution.py:32
  381.8 11.8 %cholesky.487 = f32[128,128]{1,0:T(8,128)S(1)} custom-call(f32[128,128]{1,0:T(8,128)S(1)} %cholesky.594), custom_call_target="Cholesky" | custom-call | tf_op jit(solution)/shard_map/jit(cholesky)/cholesky | solution.py:32
  394.9 9.8 %custom-call.66 = f32[1,128,128]{1,2,0:T(8,128)S(1)} custom-call(f32[1,128,128]{2,1,0:T(8,128)S(1)} %get-tuple-element.60), custom_call_target="InvertDiagBlocksLowerTriangular" | custom-call | tf_op jit(solution)/shard_map/jit(cholesky)/cholesky | solution.py:32
  408.2 11.7 %cholesky.506 = f32[128,128]{1,0:T(8,128)S(1)} custom-call(f32[128,128]{1,0:T(8,128)S(1)} %cholesky.599), custom_call_target="Cholesky" | custom-call | tf_op jit(solution)/shard_map/jit(cholesky)/cholesky | solution.py:32
  421.2 10.0 %custom-call.67 = f32[1,128,128]{1,2,0:T(8,128)S(1)} custom-call(f32[1,128,128]{2,1,0:T(8,128)S(1)} %get-tuple-element.57), custom_call_target="InvertDiagBlocksLowerTriangular" | custom-call | tf_op jit(solution)/shard_map/jit(cholesky)/cholesky | solution.py:32
  434.5 11.7 %cholesky.526 = f32[128,128]{1,0:T(8,128)S(1)} custom-call(f32[128,128]{1,0:T(8,128)S(1)} %cholesky.604), custom_call_target="Cholesky" | custom-call | tf_op jit(solution)/shard_map/jit(cholesky)/cholesky | solution.py:32
  447.5 9.8 %custom-call.68 = f32[1,128,128]{1,2,0:T(8,128)S(1)} custom-call(f32[1,128,128]{2,1,0:T(8,128)S(1)} %get-tuple-element.54), custom_call_target="InvertDiagBlocksLowerTriangular" | custom-call | tf_op jit(solution)/shard_map/jit(cholesky)/cholesky | solution.py:32
  460.3 12.1 %cholesky.546 = f32[128,128]{1,0:T(8,128)S(1)} custom-call(f32[128,128]{1,0:T(8,128)S(1)} %cholesky.609), custom_call_target="Cholesky" | custom-call | tf_op jit(solution)/shard_map/jit(cholesky)/cholesky | solution.py:32
  473.6 9.8 %custom-call.69 = f32[1,128,128]{1,2,0:T(8,128)S(1)} custom-call(f32[1,128,128]{2,1,0:T(8,128)S(1)} %get-tuple-element.51), custom_call_target="InvertDiagBlocksLowerTriangular" | custom-call | tf_op jit(solution)/shard_map/jit(cholesky)/cholesky | solution.py:32
  486.1 11.7 %cholesky.564 = f32[128,128]{1,0:T(8,128)S(1)} custom-call(f32[128,128]{1,0:T(8,128)S(1)} %convolution_subtract_fusion.13), custom_call_target="Cholesky" | custom-call | tf_op jit(solution)/shard_map/jit(cholesky)/cholesky | solution.py:32
  504.6 4.8 select_select_fusion
  509.4 22.8 %while.1 = (s32[]{:T(128)}, f32[1024,1024]{1,0:T(8,128)}, s32[8,2]{0,1:T(2,128)S(1)}, f32[8,128,128]{2,1,0:T(8,128)S(1)}, s32[]{:T(128)}) while((s32[]{:T(128)}, f32[1024,1024]{1,0:T(8,128)}, s32[8,2]{0,1:T(2,128)S(1)}, f32[8,128,128]{2,1,0:T(8,128)S(1)}, s32[]{:T(128)}) %tuple.58), condition=%wide.while_cond, body=%wide.while_body.sunk | while | flops 2 | bytes 131181 | solution.py:33
  532.3 78.8 %custom-call.70 = f32[8,128,128]{1,2,0:T(8,128)S(1)} custom-call(f32[8,128,128]{2,1,0:T(8,128)S(1)} %get-tuple-element.12), custom_call_target="InvertDiagBlocksLowerTriangular" | custom-call | tf_op jit(solution)/shard_map/jit(_solve_triangular)/triangular_solve | solution.py:33
  (107 shorter events, 86.6 us)
Async XLA Ops:
  6.5 83.8 %copy-start.1 = (bf16[768,1024]{1,0:T(8,128)(2,1)S(1)}, bf16[768,1024]{1,0:T(8,128)(2,1)}, u32[]{:S(2)}) copy-start(bf16[768,1024]{1,0:T(8,128)(2,1)} %param.8) | copy-start | bytes 4718596
  6.5 83.8 %copy-start.4 = (f32[1024]{0:T(1024)S(1)}, f32[1024]{0:T(1024)}, u32[]{:S(2)}) copy-start(f32[1024]{0:T(1024)} %param.11) | copy-start | bytes 12292
  6.5 83.8 %copy-start.3 = (f32[1024]{0:T(1024)S(1)}, f32[1024]{0:T(1024)}, u32[]{:S(2)}) copy-start(f32[1024]{0:T(1024)} %param.12) | copy-start | bytes 12292
  6.5 83.8 %copy-start.2 = (f32[4096]{0:T(1024)S(1)}, f32[4096]{0:T(1024)}, u32[]{:S(2)}) copy-start(f32[4096]{0:T(1024)} %param.14) | copy-start | bytes 49156
  6.5 83.8 %all-gather.3.cloned.1.call-start = ((), (), s32[]{:S(2)}) async-start(), calls=%async_computation | async-start | bytes 8912896 | tf_op jit(solution)/shard_map/all_gather | solution.py:18
  7.3 158.3 %all-gather.5.cloned.1.call-start = ((), (), s32[]{:S(2)}) async-start(), calls=%async_computation.1 | async-start | bytes 8912896 | tf_op jit(solution)/shard_map/all_gather | solution.py:19
  8.0 281.9 %all-reduce.3.cloned.1.call-start = ((), (), s32[]{:S(2)}) async-start(), calls=%async_computation.2 | async-start | bytes 8388608 | tf_op jit(solution)/shard_map/psum | solution.py:31
  299.7 1.9 copy-start
Sparse Core Ops, SparseCore 0:
  9.5 80.7 all-gather.2
  92.5 73.0 all-gather.4
  180.1 109.6 all-reduce.2
where the time goes:
time: 641 us; the launch traced here: 631 us
  other arithmetic  267 us (42%)
  waiting for transfers between devices  226 us (35%)
  matrix products  86.6 us (14%)
  local copies, waits for them, and re-layouts  32.5 us (5%)
  between operations  18.5 us (3%)
    another operation x30, other arithmetic, on_device(): lower = jnp.linalg.cholesky(gram)  172 us
    psum x1, waiting for transfers between devices, on_device(): gram = lax.psum(partial_gram, 'dp')  110 us
    another operation x3, other arithmetic, on_device(): jax.scipy.linalg.solve_triangular(lower, pooled.astype(jnp.float32).T, lo...  83.6 us
    all_gather x1, waiting for transfers between devices, on_device(): lax.all_gather(w_up, 'dp', axis=1, tiled=True)  77 us
    all_gather x1, waiting for transfers between devices, on_device(): lax.all_gather(w_down, 'dp', axis=1, tiled=True)  38.1 us
    dot_general x1, matrix products, on_device(): before = jnp.dot(normed, up_full, preferred_element_type=jnp.float32) + b_up  37.2 us
    another operation x14, matrix products, on_device(): lower = jnp.linalg.cholesky(gram)  23.1 us
    another operation x24, local copies, waits for them, and re-layouts  22.7 us
  transfers between devices with their start and end apart: 3, of which 3 were waited for; matrix products, arithmetic and copies ran while one was open for 7% of the time, Pallas kernels for 0%

commit v1 on v0

--- a/solution.py
+++ b/solution.py
@@ -28,7 +28,8 @@
     counts = jnp.sum(select.astype(jnp.float32), axis=1)
     pooled = (sums / jnp.maximum(counts, 1.0)[:, None]).astype(jnp.bfloat16)
     partial_gram = jnp.dot(pooled.T, pooled, preferred_element_type=jnp.float32)
-    gram = lax.psum(partial_gram, "dp")
+    terms = lax.all_gather(partial_gram, "dp")
+    gram = jnp.sum(terms, axis=0)
     lower = jnp.linalg.cholesky(gram)
     solved = jax.scipy.linalg.solve_triangular(lower, pooled.astype(jnp.float32).T, lower=True)
     total_rows = SEG_DEV * lax.axis_size("dp")

time: 641 us -> 879 us (1.37)
  waiting for transfers between devices: 226 us -> 441 us
  other arithmetic: 267 us -> 290 us
    all_gather x0 -> x1, waiting for transfers between devices: none -> 325 us  [on_device(): terms = lax.all_gather(partial_gram, 'dp')]
    psum x1 -> x0, waiting for transfers between devices: 110 us -> none  [on_device(): gram = lax.psum(partial_gram, 'dp')]
    reduce_sum x0 -> x1, other arithmetic: none -> 22.9 us  [on_device(): gram = jnp.sum(terms, axis=0)]
  transfers between devices with their start and end apart: 3 -> 3, of which waited for: 3 -> 3; matrix products, arithmetic and copies ran while one was open for 7% -> 5% of each run, Pallas kernels for 0% -> 0%
where the time goes in v1:
time: 879 us; the launch traced here: 868 us
  waiting for transfers between devices  441 us (50%)
  other arithmetic  290 us (33%)
  matrix products  86.6 us (10%)
  local copies, waits for them, and re-layouts  32.5 us (4%)
  between operations  18.5 us (2%)
    all_gather x1, waiting for transfers between devices, on_device(): terms = lax.all_gather(partial_gram, 'dp')  325 us
    another operation x30, other arithmetic, on_device(): lower = jnp.linalg.cholesky(gram)  172 us
    another operation x3, other arithmetic, on_device(): jax.scipy.linalg.solve_triangular(lower, pooled.astype(jnp.float32).T, lo...  83.6 us
    all_gather x1, waiting for transfers between devices, on_device(): lax.all_gather(w_up, 'dp', axis=1, tiled=True)  77 us
    all_gather x1, waiting for transfers between devices, on_device(): lax.all_gather(w_down, 'dp', axis=1, tiled=True)  38.1 us
    dot_general x1, matrix products, on_device(): before = jnp.dot(normed, up_full, preferred_element_type=jnp.float32) + b_up  37.2 us
    another operation x14, matrix products, on_device(): lower = jnp.linalg.cholesky(gram)  23.1 us
    reduce_sum x1, other arithmetic, on_device(): gram = jnp.sum(terms, axis=0)  22.9 us
  transfers between devices with their start and end apart: 3, of which 3 were waited for; matrix products, arithmetic and copies ran while one was open for 5% of the time, Pallas kernels for 0%

profile of v1, /device:TPU:0, one launch (start us, length us, event | category | flops | bytes accessed | tf_op | source)
XLA Modules:
  0.0 868.4 jit_solution(10103437613515064745)
XLA Ops:
  13.3 77.0 %all-gather.5.cloned.1.call-done = bf16[1024,4096]{1,0:T(8,128)(2,1)} async-done(((bf16[1024,256]{1,0:T(8,128)(2,1)}), bf16[1024,4096]{1,0:T(8,128)(2,1)}) %all-gather.5.cloned.1.call-update) | async-done | bytes 8388624 | tf_op jit(solution)/shard_map/all_gather | solution.py:18
  90.4 37.2 %fusion.2.clone.6 = bf16[768,4096]{1,0:T(8,128)(2,1)} fusion(bf16[1024,4096]{1,0:T(8,128)(2,1)} %all-gather.5.cloned.1.call-done, f32[4096]{0:T(1024)S(1)} %copy-done.2, bf16[768,1024]{1,0:T(8,128)(2,1)S(1)} %copy-done.1, f32[1024]{0:T(1024)S(1)} %copy-done.3, f32[1024]{0:T(1024)S(1)} %copy-done.4, ...), kind=kOutput, calls=%fused_computation.5.clone.clone.clone.clone.clone.1 | convolution fusion | flops 6654787584 | bytes 16283648 | tf_op jit(solution)/shard_map/dot_general | solution.py:21
  127.5 38.1 %all-gather.7.cloned.1.call-done = bf16[4096,1024]{0,1:T(8,128)(2,1)} async-done(((bf16[4096,64]{0,1:T(8,128)(2,1)}), bf16[4096,1024]{0,1:T(8,128)(2,1)}) %all-gather.7.cloned.1.call-update) | async-done | bytes 8388624 | tf_op jit(solution)/shard_map/all_gather | solution.py:19
  165.6 11.2 %fusion.49 = bf16[768,1024]{1,0:T(8,128)(2,1)S(1)} fusion(bf16[768,1024]{1,0:T(8,128)(2,1)S(1)} %copy-done.1, bf16[4096,1024]{0,1:T(8,128)(2,1)} %all-gather.7.cloned.1.call-done, bf16[768,4096]{1,0:T(8,128)(2,1)} %fusion.2.clone.6), kind=kOutput, calls=%fused_computation.66 | convolution fusion | flops 6444810240 | bytes 17825792 | tf_op jit(solution)/shard_map/dot_general | solution.py:23
  180.0 324.5 %all-gather.9.cloned.1.call-done = f32[16384,1024]{1,0:T(8,128)} async-done(((f32[1024,1024]{1,0:T(8,128)}), f32[16384,1024]{1,0:T(8,128)}) %all-gather.9.cloned.1.call-update) | async-done | bytes 67108880 | tf_op jit(solution)/shard_map/all_gather | solution.py:31
  504.6 22.9 %reduce_sum.39 = f32[1024,1024]{1,0:T(8,128)} reduce(f32[16,1024,1024]{2,1,0:T(8,128)} %bitcast, f32[]{:T(128)} %constant.305.clone.1), dimensions={0}, to_apply=%region_3.0 | reduce | flops 15728640 | bytes 71303168 | tf_op jit(solution)/shard_map/reduce_sum | solution.py:32
  527.5 5.3 copy.11
  539.2 11.7 %cholesky.223 = f32[128,128]{1,0:T(8,128)S(1)} custom-call(f32[128,128]{1,0:T(8,128)S(1)} %cholesky.580), custom_call_target="Cholesky" | custom-call | tf_op jit(solution)/shard_map/jit(cholesky)/cholesky | solution.py:33
  553.5 9.8 %custom-call.63 = f32[1,128,128]{1,2,0:T(8,128)S(1)} custom-call(f32[1,128,128]{2,1,0:T(8,128)S(1)} %get-tuple-element.69), custom_call_target="InvertDiagBlocksLowerTriangular" | custom-call | tf_op jit(solution)/shard_map/jit(cholesky)/cholesky | solution.py:33
  567.2 12.1 %cholesky.244 = f32[128,128]{1,0:T(8,128)S(1)} custom-call(f32[128,128]{1,0:T(8,128)S(1)} %cholesky.584), custom_call_target="Cholesky" | custom-call | tf_op jit(solution)/shard_map/jit(cholesky)/cholesky | solution.py:33
  580.0 9.8 %custom-call.64 = f32[1,128,128]{1,2,0:T(8,128)S(1)} custom-call(f32[1,128,128]{2,1,0:T(8,128)S(1)} %get-tuple-element.66), custom_call_target="InvertDiagBlocksLowerTriangular" | custom-call | tf_op jit(solution)/shard_map/jit(cholesky)/cholesky | solution.py:33
  593.1 11.7 %cholesky.468 = f32[128,128]{1,0:T(8,128)S(1)} custom-call(f32[128,128]{1,0:T(8,128)S(1)} %cholesky.589), custom_call_target="Cholesky" | custom-call | tf_op jit(solution)/shard_map/jit(cholesky)/cholesky | solution.py:33
  606.1 9.8 %custom-call.65 = f32[1,128,128]{1,2,0:T(8,128)S(1)} custom-call(f32[1,128,128]{2,1,0:T(8,128)S(1)} %get-tuple-element.63), custom_call_target="InvertDiagBlocksLowerTriangular" | custom-call | tf_op jit(solution)/shard_map/jit(cholesky)/cholesky | solution.py:33
  619.4 11.8 %cholesky.487 = f32[128,128]{1,0:T(8,128)S(1)} custom-call(f32[128,128]{1,0:T(8,128)S(1)} %cholesky.594), custom_call_target="Cholesky" | custom-call | tf_op jit(solution)/shard_map/jit(cholesky)/cholesky | solution.py:33
  632.6 9.8 %custom-call.66 = f32[1,128,128]{1,2,0:T(8,128)S(1)} custom-call(f32[1,128,128]{2,1,0:T(8,128)S(1)} %get-tuple-element.60), custom_call_target="InvertDiagBlocksLowerTriangular" | custom-call | tf_op jit(solution)/shard_map/jit(cholesky)/cholesky | solution.py:33
  645.8 11.7 %cholesky.506 = f32[128,128]{1,0:T(8,128)S(1)} custom-call(f32[128,128]{1,0:T(8,128)S(1)} %cholesky.599), custom_call_target="Cholesky" | custom-call | tf_op jit(solution)/shard_map/jit(cholesky)/cholesky | solution.py:33
  658.8 10.0 %custom-call.67 = f32[1,128,128]{1,2,0:T(8,128)S(1)} custom-call(f32[1,128,128]{2,1,0:T(8,128)S(1)} %get-tuple-element.57), custom_call_target="InvertDiagBlocksLowerTriangular" | custom-call | tf_op jit(solution)/shard_map/jit(cholesky)/cholesky | solution.py:33
  672.1 11.7 %cholesky.526 = f32[128,128]{1,0:T(8,128)S(1)} custom-call(f32[128,128]{1,0:T(8,128)S(1)} %cholesky.604), custom_call_target="Cholesky" | custom-call | tf_op jit(solution)/shard_map/jit(cholesky)/cholesky | solution.py:33
  685.1 9.8 %custom-call.68 = f32[1,128,128]{1,2,0:T(8,128)S(1)} custom-call(f32[1,128,128]{2,1,0:T(8,128)S(1)} %get-tuple-element.54), custom_call_target="InvertDiagBlocksLowerTriangular" | custom-call | tf_op jit(solution)/shard_map/jit(cholesky)/cholesky | solution.py:33
  697.9 12.1 %cholesky.546 = f32[128,128]{1,0:T(8,128)S(1)} custom-call(f32[128,128]{1,0:T(8,128)S(1)} %cholesky.609), custom_call_target="Cholesky" | custom-call | tf_op jit(solution)/shard_map/jit(cholesky)/cholesky | solution.py:33
  711.3 9.8 %custom-call.69 = f32[1,128,128]{1,2,0:T(8,128)S(1)} custom-call(f32[1,128,128]{2,1,0:T(8,128)S(1)} %get-tuple-element.51), custom_call_target="InvertDiagBlocksLowerTriangular" | custom-call | tf_op jit(solution)/shard_map/jit(cholesky)/cholesky | solution.py:33
  723.7 11.7 %cholesky.564 = f32[128,128]{1,0:T(8,128)S(1)} custom-call(f32[128,128]{1,0:T(8,128)S(1)} %convolution_subtract_fusion.13), custom_call_target="Cholesky" | custom-call | tf_op jit(solution)/shard_map/jit(cholesky)/cholesky | solution.py:33
  747.1 22.8 %while.1 = (s32[]{:T(128)}, f32[1024,1024]{1,0:T(8,128)}, s32[8,2]{0,1:T(2,128)S(1)}, f32[8,128,128]{2,1,0:T(8,128)S(1)}, s32[]{:T(128)}) while((s32[]{:T(128)}, f32[1024,1024]{1,0:T(8,128)}, s32[8,2]{0,1:T(2,128)S(1)}, f32[8,128,128]{2,1,0:T(8,128)S(1)}, s32[]{:T(128)}) %tuple.58), condition=%wide.while_cond, body=%wide.while_body.sunk | while | flops 2 | bytes 131181 | solution.py:34
  769.9 78.8 %custom-call.70 = f32[8,128,128]{1,2,0:T(8,128)S(1)} custom-call(f32[8,128,128]{2,1,0:T(8,128)S(1)} %get-tuple-element.12), custom_call_target="InvertDiagBlocksLowerTriangular" | custom-call | tf_op jit(solution)/shard_map/jit(_solve_triangular)/triangular_solve | solution.py:34
  (108 shorter events, 91.4 us)
Async XLA Ops:
  6.5 83.8 %copy-start.1 = (bf16[768,1024]{1,0:T(8,128)(2,1)S(1)}, bf16[768,1024]{1,0:T(8,128)(2,1)}, u32[]{:S(2)}) copy-start(bf16[768,1024]{1,0:T(8,128)(2,1)} %param.8) | copy-start | bytes 4718596
  6.5 83.8 %copy-start.4 = (f32[1024]{0:T(1024)S(1)}, f32[1024]{0:T(1024)}, u32[]{:S(2)}) copy-start(f32[1024]{0:T(1024)} %param.11) | copy-start | bytes 12292
  6.5 83.8 %copy-start.3 = (f32[1024]{0:T(1024)S(1)}, f32[1024]{0:T(1024)}, u32[]{:S(2)}) copy-start(f32[1024]{0:T(1024)} %param.12) | copy-start | bytes 12292
  6.5 83.8 %copy-start.2 = (f32[4096]{0:T(1024)S(1)}, f32[4096]{0:T(1024)}, u32[]{:S(2)}) copy-start(f32[4096]{0:T(1024)} %param.14) | copy-start | bytes 49156
  6.5 83.8 %all-gather.5.cloned.1.call-start = ((), (), s32[]{:S(2)}) async-start(), calls=%async_computation | async-start | bytes 8912896 | tf_op jit(solution)/shard_map/all_gather | solution.py:18
  7.3 158.3 %all-gather.7.cloned.1.call-start = ((), (), s32[]{:S(2)}) async-start(), calls=%async_computation.1 | async-start | bytes 8912896 | tf_op jit(solution)/shard_map/all_gather | solution.py:19
  8.0 496.5 %all-gather.9.cloned.1.call-start = ((), (), s32[]{:S(2)}) async-start(), calls=%async_computation.2 | async-start | bytes 71303168 | tf_op jit(solution)/shard_map/all_gather | solution.py:31
  537.3 1.9 copy-start
Sparse Core Ops, SparseCore 0:
  9.5 80.7 all-gather.4
  92.5 73.0 all-gather.6
  180.1 324.3 all-gather.8
